TPU v7x, 128 devices: a whole 4x4x4 slice. The times are simulated.
128 devices in a mesh: kv: 32 (over y, z, x_hi), pb: 4 (over x_lo, core).
Axes of the slice: x: 4 (x_hi: 2, x_lo: 2; x = x_hi * 2 + x_lo), y: 4, z: 4, core: 2. Of those that a mesh axis runs over, the one named last changes fastest.
Arguments:
- queries: bfloat16 [49152, 4096], P('kv', 'pb'), may hold values from -12 to 12
- cached_keys: bfloat16 [32, 256, 4096], P('kv', None, 'pb'), may hold values from -6 to 6
- cached_values: bfloat16 [32, 256, 4096], P('kv', None, 'pb'), may hold values from -6 to 6
- block_map: int32 [768, 1], P('kv'), may hold values from 0 to 31; in each aligned block of 24 rows (0 to 23, 24 to 47, ...) at most 2 rows name the same one
- out_weight: bfloat16 [4096, 4096], P('pb'), may hold values from -0.09375 to 0.09375
- hidden: bfloat16 [49152, 4096], P('kv', 'pb'), may hold values from -6 to 6
Outputs:
- mixed: bfloat16 [49152, 4096], P('kv', 'pb')
Inputs may be any that keep to these rules, and one draw needn't show every extreme that they name: `block_map`: at most 2 of the 24 spans of one index of kv name the same block, and some index has a block named by exactly 2 of its spans; every block is named by some span.
All inputs are finite; a program needn't handle non-finite values.
Results may differ from a plain program's by a relative error of at most 0.0085.
Values may be sent and summed in bfloat16 or wider, within the bound.
No kernel may reach another device: no remote copies, remote signals or barrier semaphores. Data moves between devices by JAX's collectives and lax.ppermute only.
A program may use at most 192 MiB of HBM per device.

v0:
```python
import jax
import jax.numpy as jnp
from jax import lax
from jax.sharding import PartitionSpec as P

HEAD = 128
SPAN = 64


def attend(span_queries, keys_now, values_now):
    item_count, row_count, feat_width = span_queries.shape
    key_count = keys_now.shape[0]
    head_count = feat_width // HEAD
    query_heads = span_queries.reshape(item_count, row_count, head_count, HEAD)
    key_heads = keys_now.reshape(key_count, head_count, HEAD)
    value_heads = values_now.reshape(key_count, head_count, HEAD)
    scores = jnp.einsum(
        "nrhd,khd->nhrk", query_heads, key_heads, preferred_element_type=jnp.float32
    ) * HEAD ** (-0.5)
    row_top = jnp.max(scores, axis=-1, keepdims=True)
    exponent = jnp.exp(scores - row_top)
    weights = (exponent / jnp.sum(exponent, axis=-1, keepdims=True)).astype(jnp.bfloat16)
    result = jnp.einsum("nhrk,khd->nrhd", weights, value_heads, preferred_element_type=jnp.float32)
    return result.reshape(item_count, row_count, feat_width).astype(jnp.bfloat16)


def on_device(queries, cached_keys, cached_values, block_map, out_weight, hidden):
    tok_rows, feat_width = queries.shape
    span_count = tok_rows // SPAN
    q_spans = queries.reshape(span_count, SPAN, feat_width)
    block_count = lax.axis_size("kv")
    cap_slots = max(2, span_count // block_count)
    targets = block_map[:, 0]
    onehot = (targets[:, None] == jnp.arange(block_count, dtype=jnp.int32)[None, :]).astype(
        jnp.int32
    )
    earlier = jnp.cumsum(onehot, axis=0) - onehot
    position_in = jnp.sum(earlier * onehot, axis=1)
    slot_index = targets * cap_slots + position_in
    start_sum = jnp.zeros((span_count, SPAN, feat_width), jnp.float32)
    key_piece = lax.all_gather(cached_keys, "kv", axis=0, tiled=True)
    value_piece = lax.all_gather(cached_values, "kv", axis=0, tiled=True)

    def one_block(block_step, so_far):
        keys_now = lax.dynamic_index_in_dim(key_piece, block_step, 0, keepdims=False)
        values_now = lax.dynamic_index_in_dim(value_piece, block_step, 0, keepdims=False)
        wanted = block_step * cap_slots + jnp.arange(cap_slots, dtype=jnp.int32)
        picks = (slot_index[None, :] == wanted[:, None]).astype(jnp.bfloat16)
        chosen = jnp.einsum(
            "sc,crd->srd", picks, q_spans, preferred_element_type=jnp.float32
        ).astype(jnp.bfloat16)
        answer = attend(chosen, keys_now, values_now)
        return so_far + jnp.einsum("sc,srd->crd", picks, answer, preferred_element_type=jnp.float32)

    gathered_sum = lax.fori_loop(0, key_piece.shape[0], one_block, start_sum)
    attended = gathered_sum.astype(jnp.bfloat16)
    flat_rows = attended.reshape(tok_rows, feat_width)
    partial_value = jnp.dot(flat_rows, out_weight, preferred_element_type=jnp.float32)
    summed = lax.psum_scatter(
        partial_value.astype(jnp.bfloat16), "pb", scatter_dimension=1, tiled=True
    ).astype(jnp.float32)
    return (hidden.astype(jnp.float32) + summed).astype(jnp.bfloat16)


def solution(mesh):
    placed = (
        P("kv", "pb"),
        P("kv", None, "pb"),
        P("kv", None, "pb"),
        P("kv", None),
        P("pb", None),
        P("kv", "pb"),
    )
    return jax.shard_map(
        on_device, mesh=mesh, in_specs=placed, out_specs=P("kv", "pb"), check_vma=False
    )
```

profile of v0, /device:TPU:1, one launch (start us, length us, event | category | flops | bytes accessed | tf_op | source)
XLA Modules:
  0.0 1246.2 jit_solution(3254958065707537142)
XLA Ops:
  12.7 156.4 %all-gather.5.cloned.1.call-done = bf16[32,256,1024]{2,1,0:T(8,128)(2,1)} async-done(((bf16[1,256,1024]{2,1,0:T(8,128)(2,1)}), bf16[32,256,1024]{2,1,0:T(8,128)(2,1)}) %all-gather.5.cloned.1.call-update) | async-done | bytes 16777232 | tf_op jit(solution)/shard_map/all_gather | solution.py:41
  169.1 157.2 %all-gather.3.cloned.1.call-done = bf16[32,256,1024]{2,1,0:T(8,128)(2,1)} async-done(((bf16[1,256,1024]{2,1,0:T(8,128)(2,1)}), bf16[32,256,1024]{2,1,0:T(8,128)(2,1)}) %all-gather.3.cloned.1.call-update) | async-done | bytes 16777232 | tf_op jit(solution)/shard_map/all_gather | solution.py:42
  326.2 774.2 %while.14 = (s32[]{:T(128)}, f32[24,64,1024]{2,0,1:T(8,128)}, s32[24]{0:T(128)S(1)}, bf16[32,256,1024]{2,1,0:T(8,128)(2,1)}, bf16[32,256,1024]{2,1,0:T(8,128)(2,...) while((s32[]{:T(128)}, f32[24,64,1024]{2,0,1:T(8,128)}, ...), condition=%wide.region_5.6_spmd.clone, body=%wide.region_2.5_spmd.clone.sunk | while | flops 152045168 | bytes 31465844 | solution.py:55
  338.0 4.0 fusion.55
  343.9 4.7 select_add_fusion.2
  360.3 4.0 fusion.55
  366.2 6.6 select_add_fusion.2
  384.6 4.0 fusion.55
  390.5 6.6 select_add_fusion.2
  408.8 4.0 fusion.55
  414.7 6.6 select_add_fusion.2
  433.1 4.0 fusion.55
  439.0 6.6 select_add_fusion.2
  457.3 4.0 fusion.55
  463.2 6.6 select_add_fusion.2
  481.6 4.0 fusion.55
  487.5 6.6 select_add_fusion.2
  505.8 4.0 fusion.55
  511.7 6.6 select_add_fusion.2
  530.1 4.0 fusion.55
  536.0 6.6 select_add_fusion.2
  560.2 6.6 select_add_fusion.2
  584.5 6.6 select_add_fusion.2
  608.8 6.6 select_add_fusion.2
  633.0 6.6 select_add_fusion.2
  657.3 6.6 select_add_fusion.2
  681.5 6.6 select_add_fusion.2
  705.8 6.6 select_add_fusion.2
  730.0 6.6 select_add_fusion.2
  754.3 6.6 select_add_fusion.2
  778.6 6.6 select_add_fusion.2
  802.8 6.6 select_add_fusion.2
  827.1 6.6 select_add_fusion.2
  851.3 6.6 select_add_fusion.2
  875.6 6.6 select_add_fusion.2
  899.8 6.6 select_add_fusion.2
  924.1 6.6 select_add_fusion.2
  948.3 6.6 select_add_fusion.2
  972.6 6.6 select_add_fusion.2
  996.9 6.6 select_add_fusion.2
  1021.1 6.6 select_add_fusion.2
  1045.4 6.6 select_add_fusion.2
  1069.6 6.6 select_add_fusion.2
  1093.9 6.6 select_add_fusion.2
  1100.5 6.3 copy.35
  1106.8 15.7 %convolution_convert_fusion.2 = bf16[1536,4096]{1,0:T(8,128)(2,1)} fusion(bf16[1536,1024]{1,0:T(8,128)(2,1)S(1)} %bitcast.78, bf16[1024,4096]{1,0:T(8,128)(2,1)S(1)} %copy-done.3), kind=kOutput, calls=%fused_computation.27 | convolution fusion | flops 12891193344 | bytes 24117248 | tf_op jit(solution)/shard_map/dot_general | solution.py:58
  1122.5 112.0 %reduce-scatter.2.cloned.1.call-done = bf16[1536,1024]{1,0:T(8,128)(2,1)} async-done(((bf16[1536,4096]{1,0:T(8,128)(2,1)}), bf16[1536,1024]{1,0:T(8,128)(2,1)}) %reduce-scatter.2.cloned.1.call-update) | async-done | bytes 3145744 | tf_op jit(solution)/shard_map/reduce_scatter | solution.py:59
  1234.6 5.1 add_convert_fusion
  (457 shorter events, 534.4 us)
Async XLA Ops:
  6.5 5.9 copy-start.2
  6.5 162.5 %all-gather.5.cloned.1.call-start = ((), (), s32[]{:S(2)}) async-start(), calls=%async_computation.2 | async-start | bytes 17301504 | tf_op jit(solution)/shard_map/all_gather | solution.py:41
  7.3 319.0 %all-gather.3.cloned.1.call-start = ((), (), s32[]{:S(2)}) async-start(), calls=%async_computation.1 | async-start | bytes 17301504 | tf_op jit(solution)/shard_map/all_gather | solution.py:42
  8.0 1226.5 %reduce-scatter.2.cloned.1.call-start = ((), (), s32[]{:S(2)}) async-start(), calls=%async_computation.3 | async-start | bytes 15728640 | tf_op jit(solution)/shard_map/reduce_scatter | solution.py:59
  336.6 1.0 copy-start
  359.0 1.0 copy-start
  383.2 1.0 copy-start
  407.5 1.0 copy-start
  431.7 1.0 copy-start
  456.0 1.0 copy-start
  480.2 1.0 copy-start
  504.5 1.0 copy-start
  528.7 1.0 copy-start
  553.0 1.0 copy-start
  577.3 1.0 copy-start
  601.5 1.0 copy-start
  625.8 1.0 copy-start
  650.0 1.0 copy-start
  674.3 1.0 copy-start
  698.5 1.0 copy-start
  722.8 1.0 copy-start
  747.1 1.0 copy-start
  771.3 1.0 copy-start
  795.6 1.0 copy-start
  819.8 1.0 copy-start
  844.1 1.0 copy-start
  868.3 1.0 copy-start
  892.6 1.0 copy-start
  916.8 1.0 copy-start
  941.1 1.0 copy-start
  965.3 1.0 copy-start
  989.6 1.0 copy-start
  1013.9 1.0 copy-start
  1038.1 1.0 copy-start
  1062.4 1.0 copy-start
  1086.6 1.0 copy-start
  1100.5 6.3 copy-start.3
  1122.5 112.1 %copy-start.1 = (bf16[1536,1024]{1,0:T(8,128)(2,1)S(1)}, bf16[1536,1024]{1,0:T(8,128)(2,1)}, u32[]{:S(2)}) copy-start(bf16[1536,1024]{1,0:T(8,128)(2,1)} %param.13) | copy-start | bytes 9437188
Sparse Core Ops, SparseCore 0:
  10.4 158.6 all-gather.4
  172.1 154.0 all-gather.2
  1122.6 111.8 reduce-scatter.1
where the time goes:
time: 1260 us; the launch traced here: 1250 us
  waiting for transfers between devices  427 us (34%)
  matrix products  420 us (33%)
  local copies, waits for them, and re-layouts  366 us (29%)
  other arithmetic  18.7 us (1%)
  between operations  13.1 us (1%)
    dot_general x32, matrix products, one_block(): jnp.einsum('sc,srd->crd', picks, answer, preferred_element_type=jnp.float32)  209 us
    all_gather x1, waiting for transfers between devices, on_device(): value_piece = lax.all_gather(cached_values, 'kv', axis=0, tiled=True)  157 us
    all_gather x1, waiting for transfers between devices, on_device(): key_piece = lax.all_gather(cached_keys, 'kv', axis=0, tiled=True)  156 us
    dynamic_slice x64, local copies, waits for them, and re-layouts, one_block(): lax.dynamic_index_in_dim(key_piece, block_step, 0, keepdims=False)  139 us
    dot_general x32, matrix products, attend(): jnp.einsum('nhrk,khd->nrhd', weights, value_heads, preferred_element_type...  128 us
    reduce_scatter x1, waiting for transfers between devices, on_device(): lax.psum_scatter(partial_value.astype(jnp.bfloat16), 'pb', scatter_dimens...  112 us
    dynamic_slice x32, local copies, waits for them, and re-layouts, one_block(): lax.dynamic_index_in_dim(value_piece, block_step, 0, keepdims=False)  66.1 us
    reshape x64, local copies, waits for them, and re-layouts, attend(): query_heads = span_queries.reshape(item_count, row_count, head_count, HEAD)  60.5 us
  transfers between devices with their start and end apart: 3, of which 3 were waited for; matrix products, arithmetic and copies ran while one was open for 0% of the time, Pallas kernels for 0%

commit v1 on v0

--- a/solution.py
+++ b/solution.py
@@ -39,7 +39,9 @@
     slot_index = targets * cap_slots + position_in
     start_sum = jnp.zeros((span_count, SPAN, feat_width), jnp.float32)
     key_piece = lax.all_gather(cached_keys, "kv", axis=0, tiled=True)
-    value_piece = lax.all_gather(cached_values, "kv", axis=0, tiled=True)
+    value_piece = jnp.concatenate(
+        lax.all_to_all(jnp.stack([cached_values] * lax.axis_size("kv")), "kv", 0, 0), axis=0
+    )
 
     def one_block(block_step, so_far):
         keys_now = lax.dynamic_index_in_dim(key_piece, block_step, 0, keepdims=False)

time: 1260 us -> 1330 us (1.056)
  waiting for transfers between devices: 427 us -> 498 us
    all_to_all x0 -> x1, waiting for transfers between devices: none -> 261 us  [on_device(): lax.all_to_all(jnp.stack([cached_values] * lax.axis_size('kv')), 'kv', 0, 0)]
    all_gather x1 -> x0, waiting for transfers between devices: 157 us -> none  [on_device(): value_piece = lax.all_gather(cached_values, 'kv', axis=0, tiled=True)]
    all_gather x1, waiting for transfers between devices: 156 us -> 109 us  [on_device(): key_piece = lax.all_gather(cached_keys, 'kv', axis=0, tiled=True)]
    reduce_scatter x1, waiting for transfers between devices: 112 us -> 127 us  [on_device(): lax.psum_scatter(partial_value.astype(jnp.bfloat16), 'pb', scatter_dimens...]
  transfers between devices with their start and end apart: 3 -> 3, of which waited for: 3 -> 3; matrix products, arithmetic and copies ran while one was open for 0% -> 1% of each run, Pallas kernels for 0% -> 0%
where the time goes in v1:
time: 1330 us; the launch traced here: 1320 us
  waiting for transfers between devices  498 us (37%)
  matrix products  423 us (32%)
  local copies, waits for them, and re-layouts  354 us (27%)
  other arithmetic  18 us (1%)
  between operations  13.4 us (1%)
    all_to_all x1, waiting for transfers between devices, on_device(): lax.all_to_all(jnp.stack([cached_values] * lax.axis_size('kv')), 'kv', 0, 0)  261 us
    dot_general x32, matrix products, one_block(): jnp.einsum('sc,srd->crd', picks, answer, preferred_element_type=jnp.float32)  209 us
    dot_general x32, matrix products, attend(): jnp.einsum('nhrk,khd->nrhd', weights, value_heads, preferred_element_type...  128 us
    reduce_scatter x1, waiting for transfers between devices, on_device(): lax.psum_scatter(partial_value.astype(jnp.bfloat16), 'pb', scatter_dimens...  127 us
    dynamic_slice x64, local copies, waits for them, and re-layouts, one_block(): lax.dynamic_index_in_dim(key_piece, block_step, 0, keepdims=False)  125 us
    all_gather x1, waiting for transfers between devices, on_device(): key_piece = lax.all_gather(cached_keys, 'kv', axis=0, tiled=True)  109 us
    convert_element_type x64, local copies, waits for them, and re-layouts, attend(): result.reshape(item_count, row_count, feat_width).astype(jnp.bfloat16)  60.5 us
    reshape x64, local copies, waits for them, and re-layouts, attend(): query_heads = span_queries.reshape(item_count, row_count, head_count, HEAD)  60.5 us
  transfers between devices with their start and end apart: 3, of which 3 were waited for; matrix products, arithmetic and copies ran while one was open for 1% of the time, Pallas kernels for 0%

profile of v1, /device:TPU:1, one launch (start us, length us, event | category | flops | bytes accessed | tf_op | source)
XLA Modules:
  0.0 1318.9 jit_solution(1254690653540541889)
XLA Ops:
  8.5 5.9 stack.2
  14.4 11.6 all-to-all-start
  30.0 261.2 %all-to-all-done = bf16[32,1,256,1024]{2,3,1,0:T(8,128)(2,1)} async-done(((bf16[32,1,256,1024]{2,3,1,0:T(8,128)(2,1)}), bf16[32,1,256,1024]{2,3,1,0:T(8,128)(2,1)}, u32[]{:S(2)}, u32[]{:S(2)}) %all-to-all-start) | async-done | bytes 16777248 | tf_op jit(solution)/shard_map/all_to_all | solution.py:43
  291.3 108.9 %all-gather.2.cloned.1.call-done = bf16[32,256,1024]{2,1,0:T(8,128)(2,1)} async-done(((bf16[1,256,1024]{2,1,0:T(8,128)(2,1)}), bf16[32,256,1024]{2,1,0:T(8,128)(2,1)}) %all-gather.2.cloned.1.call-update) | async-done | bytes 16777232 | tf_op jit(solution)/shard_map/all_gather | solution.py:41
  400.1 754.6 %while.14 = (s32[]{:T(128)}, f32[24,64,1024]{2,0,1:T(8,128)}, s32[24]{0:T(128)S(1)}, bf16[32,256,1024]{1,2,0:T(8,128)(2,1)}, bf16[32,256,1024]{2,1,0:T(8,128)(2,...) while((s32[]{:T(128)}, f32[24,64,1024]{2,0,1:T(8,128)}, ...), condition=%wide.region_5.6_spmd.clone, body=%wide.region_2.5_spmd.clone.sunk | while | flops 152045168 | bytes 30417264 | solution.py:57
  411.3 4.0 fusion.55
  417.2 4.7 select_add_fusion.2
  433.0 4.0 fusion.55
  438.9 6.6 select_add_fusion.2
  456.6 4.0 fusion.55
  462.5 6.6 select_add_fusion.2
  480.3 4.0 fusion.55
  486.2 6.6 select_add_fusion.2
  503.9 4.0 fusion.55
  509.8 6.6 select_add_fusion.2
  527.6 4.0 fusion.55
  533.5 6.6 select_add_fusion.2
  551.2 4.0 fusion.55
  557.1 6.6 select_add_fusion.2
  580.7 6.6 select_add_fusion.2
  604.4 6.6 select_add_fusion.2
  628.0 6.6 select_add_fusion.2
  651.7 6.6 select_add_fusion.2
  675.3 6.6 select_add_fusion.2
  698.9 6.6 select_add_fusion.2
  722.6 6.6 select_add_fusion.2
  746.2 6.6 select_add_fusion.2
  769.9 6.6 select_add_fusion.2
  793.5 6.6 select_add_fusion.2
  817.1 6.6 select_add_fusion.2
  840.8 6.6 select_add_fusion.2
  864.4 6.6 select_add_fusion.2
  888.1 6.6 select_add_fusion.2
  911.7 6.6 select_add_fusion.2
  935.3 6.6 select_add_fusion.2
  959.0 6.6 select_add_fusion.2
  982.6 6.6 select_add_fusion.2
  1006.3 6.6 select_add_fusion.2
  1029.9 6.6 select_add_fusion.2
  1053.5 6.6 select_add_fusion.2
  1077.2 6.6 select_add_fusion.2
  1100.8 6.6 select_add_fusion.2
  1124.5 6.6 select_add_fusion.2
  1148.1 6.6 select_add_fusion.2
  1154.7 6.1 copy.34
  1160.8 18.8 %convolution_convert_fusion.2 = bf16[1536,4096]{1,0:T(8,128)(2,1)} fusion(bf16[1536,1024]{1,0:T(8,128)(2,1)S(1)} %bitcast.80, bf16[1024,4096]{1,0:T(8,128)(2,1)} %param.12), kind=kOutput, calls=%fused_computation.27 | convolution fusion | flops 12891193344 | bytes 24117248 | tf_op jit(solution)/shard_map/dot_general | solution.py:60
  1179.6 127.3 %reduce-scatter.2.cloned.1.call-done = bf16[1536,1024]{1,0:T(8,128)(2,1)} async-done(((bf16[1536,4096]{1,0:T(8,128)(2,1)}), bf16[1536,1024]{1,0:T(8,128)(2,1)}) %reduce-scatter.2.cloned.1.call-update) | async-done | bytes 3145744 | tf_op jit(solution)/shard_map/reduce_scatter | solution.py:61
  1306.9 5.1 add_convert_fusion
  (456 shorter events, 522.9 us)
Async XLA Ops:
  6.5 393.6 %all-gather.2.cloned.1.call-start = ((), (), s32[]{:S(2)}) async-start(), calls=%async_computation.2 | async-start | bytes 17301504 | tf_op jit(solution)/shard_map/all_gather | solution.py:41
  14.4 11.7 copy-start.2
  14.4 276.8 %all-to-all-start = ((bf16[32,1,256,1024]{2,3,1,0:T(8,128)(2,1)}), bf16[32,1,256,1024]{2,3,1,0:T(8,128)(2,1)}, u32[]{:S(2)}, u32[]{:S(2)}) async-start(bf16[32,1,256,1024]{2,3,1,0:T(8,128)(2,1)} %stack.2), calls=%async_computation | async-start | bytes 33554432 | tf_op jit(solution)/shard_map/all_to_all | solution.py:43
  26.0 1280.9 %reduce-scatter.2.cloned.1.call-start = ((), (), s32[]{:S(2)}) async-start(), calls=%async_computation.3 | async-start | bytes 15728640 | tf_op jit(solution)/shard_map/reduce_scatter | solution.py:61
  408.1 1.0 copy-start
  429.8 1.0 copy-start
  453.4 1.0 copy-start
  477.0 1.0 copy-start
  500.7 1.0 copy-start
  524.3 1.0 copy-start
  548.0 1.0 copy-start
  571.6 1.0 copy-start
  595.2 1.0 copy-start
  618.9 1.0 copy-start
  642.5 1.0 copy-start
  666.2 1.0 copy-start
  689.8 1.0 copy-start
  713.4 1.0 copy-start
  737.1 1.0 copy-start
  760.7 1.0 copy-start
  784.4 1.0 copy-start
  808.0 1.0 copy-start
  831.7 1.0 copy-start
  855.3 1.0 copy-start
  878.9 1.0 copy-start
  902.6 1.0 copy-start
  926.2 1.0 copy-start
  949.9 1.0 copy-start
  973.5 1.0 copy-start
  997.1 1.0 copy-start
  1020.8 1.0 copy-start
  1044.4 1.0 copy-start
  1068.1 1.0 copy-start
  1091.7 1.0 copy-start
  1115.3 1.0 copy-start
  1139.0 1.0 copy-start
  1179.6 127.3 %copy-start.1 = (bf16[1536,1024]{1,0:T(8,128)(2,1)S(1)}, bf16[1536,1024]{1,0:T(8,128)(2,1)}, u32[]{:S(2)}) copy-start(bf16[1536,1024]{1,0:T(8,128)(2,1)} %param.13) | copy-start | bytes 9437188
Sparse Core Ops, SparseCore 0:
  10.4 389.6 all-gather.1
  1179.7 127.1 reduce-scatter.1
